TPU v7x, 32 devices: a whole 2x2x4 slice. The times are simulated.
32 devices in a mesh: clips: 2 (over y), row: 4 (over x, core), col: 4 (over z).
Axes of the slice: x: 2, y: 2, z: 4, core: 2. Of those that a mesh axis runs over, the one named last changes fastest.
Arguments:
- clip_tokens: bfloat16 [2048, 6144], P(('clips', 'col'), 'row'), parts along dimension 0, may hold values from -12 to 12
- modulation: float32 [8, 6, 6144], P('clips', None, 'row'), parts along dimension 0, may hold values from -3 to 3
- w_qkv: bfloat16 [6144, 3, 4096], P('row', None, 'col'), may hold values from -3 to 3
- w_out: bfloat16 [4096, 6144], P('col', 'row'), may hold values from -0.09375 to 0.09375
- w_up: bfloat16 [6144, 12288], P('row', 'col'), may hold values from -0.078125 to 0.078125
- up_bias: float32 [12288], P('col'), may hold values from -3 to 3
- w_down: bfloat16 [12288, 6144], P('col', 'row'), may hold values from -0.0546875 to 0.0546875
- guide_num: int32 [8], P('clips'), parts along dimension 0, may hold values from -3 to 10, as said below
Outputs:
- guided: bfloat16 [512, 6144], P(('clips', 'col'), 'row'), parts along dimension 0
There are 2 independent parts, one for each index of `clips`. A program takes and returns all parts, laid end to end along the dimension named above; an argument that names none is the same for every part. Nothing has to cross between parts.
Inputs may be any that keep to these rules, and one draw needn't show every extreme that they name: `guide_num`: the three negative numerators are -1, -2 and -3 in some order, and the positive one makes the four sum to 4.
All inputs are finite; a program needn't handle non-finite values.
Results may differ from a plain program's by a relative error of at most 0.019.
Values may be sent and summed in bfloat16 or wider, within the bound.
A program may use at most 128 MiB of HBM per device.

v0:
```python
import jax
import jax.numpy as jnp
from jax import lax
from jax.sharding import PartitionSpec as P

D = 6144
HEAD_DIM = 128
eps = 1e-06


def normalize(values, shift, scale):
    totals = lax.psum((jnp.sum(values, axis=1), jnp.sum(values * values, axis=1)), "row")
    mean = totals[0] / D
    variance = totals[1] / D - mean * mean
    normed = (values - mean[:, None]) * lax.rsqrt(variance + eps)[:, None]
    branches = shift.shape[0]
    shaped = normed.reshape(-1, branches, values.shape[1]) * (1.0 + scale[None]) + shift[None]
    return shaped.reshape(values.shape)


def general_layer(clip_tokens, modulation, w_qkv, w_out, w_up, up_bias, w_down, guide_num):
    branches = modulation.shape[0]
    feat_rows = w_qkv.shape[0]
    head_cols = w_qkv.shape[2]
    heads_here = head_cols // HEAD_DIM
    x_rows = clip_tokens.astype(jnp.float32)
    first = normalize(x_rows, modulation[:, 0], modulation[:, 1]).astype(jnp.bfloat16)
    w_flat = w_qkv.reshape(feat_rows, 3 * head_cols)
    partial_qkv = jnp.dot(
        lax.all_gather(first, "col", axis=0, tiled=True), w_flat, preferred_element_type=jnp.float32
    )
    scale_score = 1.0 / jnp.sqrt(jnp.float32(HEAD_DIM))
    qkv = lax.psum_scatter(partial_qkv.astype(jnp.bfloat16), "row", scatter_dimension=0, tiled=True)
    query3 = qkv[:, :head_cols].reshape(-1, heads_here, HEAD_DIM)
    query_rows = query3.shape[0]
    piece = (
        lax.all_gather(qkv[:, head_cols : 2 * head_cols], "row", axis=0, tiled=True),
        lax.all_gather(qkv[:, 2 * head_cols :], "row", axis=0, tiled=True),
    )
    top = jnp.full((heads_here, query_rows), -1e30, jnp.float32)
    rows = piece[0].shape[0]
    key_heads = piece[0].reshape(rows, heads_here, HEAD_DIM)
    value_heads = piece[1].reshape(rows, heads_here, HEAD_DIM)
    scores = (
        jnp.einsum("qhd,khd->hqk", query3, key_heads, preferred_element_type=jnp.float32)
        * scale_score
    )
    query_branch = jnp.arange(query3.shape[0], dtype=jnp.int32) % branches
    key_branch = jnp.arange(rows, dtype=jnp.int32) % branches
    allowed = (query_branch[:, None] == key_branch[None, :])[None]
    masked = jnp.where(allowed, scores, -1e30)
    new_top = jnp.maximum(top, jnp.max(masked, axis=-1))
    weights = jnp.where(allowed, jnp.exp(masked - new_top[..., None]), 0.0)
    denom = jnp.sum(weights, axis=-1)
    accum = jnp.einsum(
        "hqk,khd->hqd",
        weights.astype(jnp.bfloat16),
        value_heads,
        preferred_element_type=jnp.float32,
    )
    att = (accum / denom[..., None]).transpose(1, 0, 2).reshape(-1, head_cols).astype(jnp.bfloat16)
    partial_out = jnp.dot(
        lax.all_gather(att, "row", axis=0, tiled=True), w_out, preferred_element_type=jnp.float32
    )
    out_rows = lax.psum_scatter(
        partial_out.astype(jnp.bfloat16), "col", scatter_dimension=0, tiled=True
    ).astype(jnp.float32)
    by_branch = x_rows.shape[0] // branches
    resid = (
        x_rows.reshape(by_branch, branches, feat_rows)
        + modulation[None, :, 2] * out_rows.reshape(by_branch, branches, feat_rows)
    ).reshape(x_rows.shape)
    second = normalize(resid, modulation[:, 3], modulation[:, 4]).astype(jnp.bfloat16)
    partial_up = jnp.dot(
        lax.all_gather(second, "col", axis=0, tiled=True), w_up, preferred_element_type=jnp.float32
    )
    up_rows = lax.psum_scatter(
        partial_up.astype(jnp.bfloat16), "row", scatter_dimension=0, tiled=True
    ).astype(jnp.float32)
    act = jax.nn.gelu(up_rows + up_bias[None], approximate=True).astype(jnp.bfloat16)
    partial_down = jnp.dot(
        lax.all_gather(act, "row", axis=0, tiled=True), w_down, preferred_element_type=jnp.float32
    )
    guide_weights = guide_num.astype(jnp.float32) / 4.0
    weights_gate = guide_weights[:, None] * modulation[:, 5]
    combined = jnp.sum(partial_down.reshape(-1, branches, feat_rows) * weights_gate[None], axis=1)
    mlp_rows = lax.psum_scatter(
        combined.astype(jnp.bfloat16), "col", scatter_dimension=0, tiled=True
    ).astype(jnp.float32)
    resid_mix = jnp.sum(
        resid.reshape(by_branch, branches, feat_rows) * guide_weights[None, :, None], axis=1
    )
    return (resid_mix + mlp_rows).astype(jnp.bfloat16)


BF = jnp.bfloat16


def swap_row(value, distance):
    size = lax.axis_size("row")
    return lax.ppermute(value, "row", [(r, r ^ distance) for r in range(size)])


def sum_over_row(value):
    value = value + swap_row(value, 1)
    return value + swap_row(value, 2)


def scatter_row(partial, axis):
    me = lax.axis_index("row")
    half, core = (me // 2, me % 2)
    span = partial.shape[axis] // 4

    def piece(index):
        return lax.dynamic_slice_in_dim(partial, index * span, span, axis)

    far = swap_row(piece((1 - half) * 2 + 1 - core), 1)
    near = swap_row(piece(half * 2 + 1 - core), 1)
    away = piece((1 - half) * 2 + core).astype(jnp.float32) + far.astype(jnp.float32)
    came = swap_row(away.astype(BF), 2)
    kept = piece(half * 2 + core).astype(jnp.float32) + near.astype(jnp.float32)
    return kept + came.astype(jnp.float32)


def shift_col(value, distance):
    size = lax.axis_size("col")
    return lax.ppermute(value, "col", [(c, (c + distance) % size) for c in range(size)])


def gather_col(value):
    size = lax.axis_size("col")
    return jnp.stack([value] + [shift_col(value, k) for k in range(1, size)])


def in_order(blocks):
    size, me = (blocks.shape[0], lax.axis_index("col"))
    return jnp.stack(
        [lax.dynamic_index_in_dim(blocks, (me - k) % size, 0, False) for k in range(size)]
    )


def gather_row(value, other, axis):
    me = lax.axis_index("row")
    half, core = (me // 2, me % 2)
    beside = swap_row(value, 1)
    across = swap_row(other, 1)

    def pick(x, c):
        same = jnp.where(core == c, value, beside)
        away = jnp.where(core == c, other, across)
        return jnp.where(half == x, same, away)

    return jnp.concatenate([pick(0, 0), pick(0, 1), pick(1, 0), pick(1, 1)], axis=axis)


def apply_norm(values, totals, shift, scale):
    totals = totals.reshape(2, *values.shape[:3])
    mean = totals[0] / D
    variance = totals[1] / D - mean * mean
    normed = (values - mean[..., None]) * lax.rsqrt(variance + eps)[..., None]
    return (normed * (1.0 + scale[None, :, None]) + shift[None, :, None]).astype(BF)


def moments(values):
    return jnp.stack([jnp.sum(values, axis=-1), jnp.sum(values * values, axis=-1)]).reshape(2, -1)


def attend(q, k, v):
    scores = jnp.einsum("bhqd,bhkd->bhqk", q, k, preferred_element_type=jnp.float32)
    scores = scores / jnp.sqrt(jnp.float32(HEAD_DIM))
    weights = jnp.exp(scores - jnp.max(scores, axis=-1, keepdims=True))
    denom = jnp.sum(weights, axis=-1)
    mixed = jnp.einsum("bhqk,bhkd->bhqd", weights.astype(BF), v, preferred_element_type=jnp.float32)
    return (mixed / denom[..., None]).astype(BF)


GROUPS = 2


def head_layer(clip_tokens, modulation, w_qkv, w_out, w_up, up_bias, w_down, guide_num):
    branches = modulation.shape[0]
    feat_rows, _, head_cols = w_qkv.shape
    mine = head_cols // 4
    heads = mine // HEAD_DIM
    here = clip_tokens.shape[0] // branches
    wide = branches // GROUPS
    cols = lax.axis_size("col")
    w_flat = w_qkv.reshape(feat_rows, 3, 4, mine).transpose(0, 2, 1, 3).reshape(feat_rows, -1)
    by_branch = clip_tokens.reshape(here, branches, feat_rows).transpose(1, 0, 2)
    guide = guide_num.astype(jnp.float32) / 4.0
    gate = guide[:, None] * modulation[:, 5]
    parts = [slice(g * wide, (g + 1) * wide) for g in range(GROUPS)]
    tokens = cols * wide * here
    x_parts = [by_branch[p].reshape(wide * here, feat_rows) for p in parts]
    gathered = [lax.all_gather(x, "col", axis=0, tiled=True) for x in x_parts]
    gathered[0], w_flat = lax.optimization_barrier((gathered[0], w_flat))

    def project(g):
        mod = modulation[parts[g]]
        x_all = gathered[g].astype(jnp.float32).reshape(cols, wide, here, feat_rows)
        first = apply_norm(x_all, sum_over_row(moments(x_all)), mod[:, 0], mod[:, 1])
        first = first.reshape(tokens, feat_rows)
        partial = jnp.dot(first, w_flat, preferred_element_type=jnp.float32).astype(BF)
        return scatter_row(partial, 1).astype(BF)

    def attention(g, qkv):
        shaped = qkv.reshape(cols, wide, here, 3, heads, HEAD_DIM).transpose(3, 1, 4, 0, 2, 5)
        shaped = shaped.reshape(3, wide, heads, cols * here, HEAD_DIM)
        att = attend(shaped[0], shaped[1], shaped[2])
        att = att.reshape(wide, heads, cols, here, HEAD_DIM).transpose(2, 0, 3, 1, 4)
        att = att.reshape(tokens, mine)
        att_all = gather_row(att, swap_row(att, 2), 1)
        partial = jnp.dot(att_all, w_out, preferred_element_type=jnp.float32).astype(BF)
        return lax.psum_scatter(partial, "col", scatter_dimension=0, tiled=True)

    def residual(g, out):
        mod = modulation[parts[g]]
        x = x_parts[g].astype(jnp.float32).reshape(1, wide, here, feat_rows)
        out = out.astype(jnp.float32).reshape(1, wide, here, feat_rows)
        resid = x + mod[None, :, 2, None] * out
        second = apply_norm(resid, sum_over_row(moments(resid)), mod[:, 3], mod[:, 4])
        second = second.reshape(wide * here, feat_rows)
        mixed = jnp.sum(resid[0] * guide[parts[g]][:, None, None], axis=0)
        if g:
            seconds[-1], second = lax.optimization_barrier((seconds[-1], second))
        if g < GROUPS - 1:
            return (mixed, gather_col(second).reshape(tokens, feat_rows))
        return (mixed, lax.all_gather(second, "col", axis=0, tiled=True))

    def expand(g, second_all):
        partial = jnp.dot(second_all, w_up, preferred_element_type=jnp.float32).astype(BF)
        if g:
            before = acts[g - 1]
            partial, other = lax.optimization_barrier((partial, before[1]))
            acts[g - 1] = (before[0], other)
        up = scatter_row(partial, 0)
        act = jax.nn.gelu(up + up_bias[None], approximate=True).astype(BF)
        return (act, swap_row(act, 2))

    def contract(g, act):
        down = jnp.dot(gather_row(act[0], act[1], 0), w_down, preferred_element_type=jnp.float32)
        down = down.reshape(cols, wide, here, feat_rows)
        down = sum((down[:, b] * gate[parts[g]][b] for b in range(wide)))
        return in_order(down) if g < GROUPS - 1 else down

    every = range(GROUPS)
    qkv, acts = ([], [])
    for g in every:
        if g:
            gathered[g], qkv[-1] = lax.optimization_barrier((gathered[g], qkv[-1]))
        qkv.append(project(g))
    outs = [attention(g, qkv[g]) for g in every]
    mixed, seconds = ([], [])
    for g in every:
        out = outs[g]
        if g:
            out, seconds[-1] = lax.optimization_barrier((out, seconds[-1]))
        kept, second = residual(g, out)
        mixed.append(kept)
        seconds.append(second)
    for g in every:
        second = seconds[g]
        if g:
            second, act = lax.optimization_barrier((second, acts[-1][0]))
            acts[-1] = (act, acts[-1][1])
        acts.append(expand(g, second))
    total = sum((contract(g, acts[g]) for g in every))
    total = total.astype(BF).reshape(cols * here, feat_rows)
    mlp = lax.psum_scatter(total, "col", scatter_dimension=0, tiled=True)
    return (sum(mixed) + mlp.astype(jnp.float32)).astype(BF)


def on_device(*args):
    heads_here = args[2].shape[2] // HEAD_DIM
    if lax.axis_size("row") == 4 and heads_here % 4 == 0:
        return head_layer(*args)
    return general_layer(*args)


def solution(mesh):
    in_specs = (
        P(("clips", "col"), "row"),
        P("clips", None, "row"),
        P("row", None, "col"),
        P("col", "row"),
        P("row", "col"),
        P("col"),
        P("col", "row"),
        P("clips"),
    )
    out_specs = P(("clips", "col"), "row")
    return jax.shard_map(
        on_device, mesh=mesh, in_specs=in_specs, out_specs=out_specs, check_vma=False
    )
```

profile of v0, /device:TPU:0, one launch (start us, length us, event | category | flops | bytes accessed | tf_op | source)
XLA Modules:
  0.0 391.4 jit_solution(15030035954881024947)
XLA Ops:
  6.5 2.5 reshape.357
  12.3 12.6 %copy.32 = bf16[1536,3,1024]{0,2,1:T(8,128)(2,1)} copy(bf16[1536,3,1024]{2,0,1:T(8,128)(2,1)} %param.10) | data formatting | bytes 18874368 | tf_op args[2]
  24.9 8.0 %copy.33 = bf16[1536,4,3,256]{0,3,2,1:T(8,128)(2,1)} copy(bf16[1536,4,3,256]{0,3,1,2:T(8,128)(2,1)} %bitcast.146) | data formatting | bytes 18874368 | tf_op jit(solution)/shard_map/transpose | solution.py:188
  32.9 19.3 %all-gather.6.cloned.1.call-done = bf16[512,1536]{1,0:T(8,128)(2,1)} async-done(((bf16[128,1536]{1,0:T(8,128)(2,1)}), bf16[512,1536]{1,0:T(8,128)(2,1)}) %all-gather.6.cloned.1.call-update) | async-done | bytes 1572880 | tf_op jit(solution)/shard_map/all_gather | solution.py:195
  59.1 2.7 fusion.4
  61.8 9.6 %convolution_convert_fusion.3 = bf16[512,3072]{1,0:T(8,128)(2,1)S(1)} fusion(bf16[512,1536]{1,0:T(8,128)(2,1)S(1)} %fusion.4, bf16[1536,3072]{0,1:T(8,128)(2,1)} %bitcast.152), kind=kOutput, calls=%fused_computation.9 | convolution fusion | flops 4833411072 | bytes 14155776 | tf_op jit(solution)/shard_map/dot_general | solution.py:203
  76.2 2.5 add_convert_fusion.5
  80.2 18.4 %collective-permute-done.4 = bf16[512,768]{1,0:T(8,128)(2,1)} collective-permute-done((bf16[512,768]{1,0:T(8,128)(2,1)}, bf16[512,768]{1,0:T(8,128)(2,1)}, u32[]{:S(2)}, u32[]{:S(2)}) %collective-permute-start.4) | collective-permute-done | bytes 786464 | tf_op jit(solution)/shard_map/ppermute | solution.py:101
  98.6 2.8 add_convert_fusion.4
  101.4 2.7 reshape.362
  112.8 9.1 %convolution_convert_fusion.2 = bf16[512,3072]{1,0:T(8,128)(2,1)S(1)} fusion(bf16[512,1536]{1,0:T(8,128)(2,1)S(1)} %fusion.9, bf16[1536,3072]{0,1:T(8,128)(2,1)} %bitcast.153), kind=kOutput, calls=%fused_computation.8 | convolution fusion | flops 4833411072 | bytes 14155776 | tf_op jit(solution)/shard_map/dot_general | solution.py:203
  128.7 2.4 add_convert_fusion.3
  132.6 3.0 convolution_convert_fusion.5
  135.6 15.4 %collective-permute-done.12 = bf16[512,768]{1,0:T(8,128)(2,1)} collective-permute-done((bf16[512,768]{1,0:T(8,128)(2,1)}, bf16[512,768]{1,0:T(8,128)(2,1)}, u32[]{:S(2)}, u32[]{:S(2)}) %collective-permute-start.12) | collective-permute-done | bytes 786464 | tf_op jit(solution)/shard_map/ppermute | solution.py:101
  151.0 2.8 add_convert_fusion.2
  153.8 2.9 reshape.367
  161.3 6.1 %collective-permute-done.14 = bf16[512,256]{1,0:T(8,128)(2,1)S(1)} collective-permute-done((bf16[512,256]{1,0:T(8,128)(2,1)S(1)}, bf16[512,256]{1,0:T(8,128)(2,1)S(1)}, u32[]{:S(2)}, u32[]{:S(2)}) %collective-permute-start.14) | collective-permute-done | bytes 262176 | tf_op jit(solution)/shard_map/ppermute | solution.py:101
  169.0 3.0 convolution_convert_fusion.4
  183.1 2.2 collective-permute-start.20
  185.3 17.9 %collective-permute-done.18 = bf16[128,1536]{1,0:T(8,128)(2,1)S(1)} collective-permute-done((bf16[128,1536]{1,0:T(8,128)(2,1)S(1)}, bf16[128,1536]{1,0:T(8,128)(2,1)S(1)}, u32[]{:S(2)}, u32[]{:S(2)}) %collective-permute-start.18) | collective-permute-done | bytes 393248 | tf_op jit(solution)/shard_map/ppermute | solution.py:127
  203.3 26.2 %collective-permute-done.19 = bf16[128,1536]{1,0:T(8,128)(2,1)S(1)} collective-permute-done((bf16[128,1536]{1,0:T(8,128)(2,1)S(1)}, bf16[128,1536]{1,0:T(8,128)(2,1)S(1)}, u32[]{:S(2)}, u32[]{:S(2)}) %collective-permute-start.19) | collective-permute-done | bytes 393248 | tf_op jit(solution)/shard_map/ppermute | solution.py:127
  240.2 8.1 %convolution_convert_fusion.1 = bf16[512,3072]{1,0:T(8,128)(2,1)S(1)} fusion(bf16[512,1536]{1,0:T(8,128)(2,1)} %bitcast.162, bf16[1536,3072]{1,0:T(8,128)(2,1)} %param.12), kind=kOutput, calls=%fused_computation.7 | convolution fusion | flops 4833411072 | bytes 14155776 | tf_op jit(solution)/shard_map/dot_general | solution.py:231
  252.2 2.2 add_convert_fusion.1
  255.9 18.4 %collective-permute-done.25 = bf16[128,3072]{1,0:T(8,128)(2,1)} collective-permute-done((bf16[128,3072]{1,0:T(8,128)(2,1)}, bf16[128,3072]{1,0:T(8,128)(2,1)}, u32[]{:S(2)}, u32[]{:S(2)}) %collective-permute-start.25) | collective-permute-done | bytes 786464 | tf_op jit(solution)/shard_map/ppermute | solution.py:101
  274.3 3.1 fusion.33
  278.8 16.8 %all-gather.8.cloned.1.call-done = bf16[512,1536]{1,0:T(8,128)(2,1)} async-done(((bf16[128,1536]{1,0:T(8,128)(2,1)}), bf16[512,1536]{1,0:T(8,128)(2,1)}) %all-gather.8.cloned.1.call-update) | async-done | bytes 1572880 | tf_op jit(solution)/shard_map/all_gather | solution.py:228
  295.7 8.3 %convolution_convert_fusion = bf16[512,3072]{1,0:T(8,128)(2,1)S(1)} fusion(bf16[512,1536]{1,0:T(8,128)(2,1)} %all-gather.8.cloned.1.call-done, bf16[1536,3072]{1,0:T(8,128)(2,1)} %param.12), kind=kOutput, calls=%fused_computation.6 | convolution fusion | flops 4833411072 | bytes 14155776 | tf_op jit(solution)/shard_map/dot_general | solution.py:231
  312.6 16.3 %collective-permute-done.31 = bf16[128,3072]{1,0:T(8,128)(2,1)S(1)} collective-permute-done((bf16[128,3072]{1,0:T(8,128)(2,1)S(1)}, bf16[128,3072]{1,0:T(8,128)(2,1)S(1)}, u32[]{:S(2)}, u32[]{:S(2)}) %collective-permute-start.31) | collective-permute-done | bytes 786464 | tf_op jit(solution)/shard_map/ppermute | solution.py:101
  331.2 8.9 %fusion.10 = f32[512,1536]{1,0:T(8,128)S(1)} fusion(bf16[3072,1536]{1,0:T(8,128)(2,1)} %param.14, bf16[128,3072]{1,0:T(8,128)(2,1)S(1)} %get-tuple-element.48, bf16[128,3072]{1,0:T(8,128)(2,1)S(1)} %get-tuple-element.49, bf16[128,3072]{1,0:T(8,128)(2,1)S(1)} %get-tuple-element.50, bf16[128,3072]{1,0:T(8,128)(2,1)S(1)} %get-tuple-element.47), kind=kOutput, calls=%fused_computation.20 | convolution fusion | flops 4844421120 | bytes 15728640 | tf_op jit(solution)/shard_map/dot_general | solution.py:241
  340.1 8.3 %collective-permute-done.33 = bf16[128,3072]{1,0:T(8,128)(2,1)S(1)} collective-permute-done((bf16[128,3072]{1,0:T(8,128)(2,1)S(1)}, bf16[128,3072]{1,0:T(8,128)(2,1)S(1)}, u32[]{:S(2)}, u32[]{:S(2)}) %collective-permute-start.33) | collective-permute-done | bytes 786464 | tf_op jit(solution)/shard_map/ppermute | solution.py:101
  351.1 5.0 %fusion.18 = f32[512,1536]{1,0:T(8,128)S(1)} fusion(bf16[3072,1536]{1,0:T(8,128)(2,1)S(1)} %bitcast.204, bf16[128,3072]{1,0:T(8,128)(2,1)S(1)} %get-tuple-element.54, bf16[128,3072]{1,0:T(8,128)(2,1)S(1)} %get-tuple-element.55, bf16[128,3072]{1,0:T(8,128)(2,1)S(1)} %get-tuple-element.56, bf16[128,3072]{1,0:T(8,128)(2,1)S(1)} %get-tuple-element.53), kind=kOutput, calls=%fused_computation.28 | convolution fusion | flops 4844421120 | bytes 15728640 | tf_op jit(solution)/shard_map/dot_general | solution.py:241
  357.8 24.6 %reduce-scatter.8.cloned.1.call-done = bf16[64,1536]{1,0:T(8,128)(2,1)} async-done(((bf16[256,1536]{1,0:T(8,128)(2,1)}), bf16[64,1536]{1,0:T(8,128)(2,1)}) %reduce-scatter.8.cloned.1.call-update) | async-done | bytes 196624 | tf_op jit(solution)/shard_map/reduce_scatter | solution.py:269
  (190 shorter events, 85.1 us)
Async XLA Ops:
  6.5 45.6 %all-gather.6.cloned.1.call-start = ((), (), s32[]{:S(2)}) async-start(), calls=%async_computation.4 | async-start | bytes 1966080 | tf_op jit(solution)/shard_map/all_gather | solution.py:195
  12.2 89.2 %all-gather.4.cloned.1.call-start = ((), (), s32[]{:S(2)}) async-start(), calls=%async_computation.3 | async-start | bytes 1966080 | tf_op jit(solution)/shard_map/all_gather | solution.py:195
  54.3 118.4 %reduce-scatter.4.cloned.1.call-start = ((), (), s32[]{:S(2)}) async-start(), calls=%async_computation.5 | async-start | bytes 1966080 | tf_op jit(solution)/shard_map/reduce_scatter | solution.py:214
  55.4 3.7 collective-permute-start.1
  73.6 6.6 %collective-permute-start.2 = (bf16[512,768]{1,0:T(8,128)(2,1)}, bf16[512,768]{1,0:T(8,128)(2,1)}, u32[]{:S(2)}, u32[]{:S(2)}) collective-permute-start(bf16[512,768]{1,0:T(8,128)(2,1)} %get-tuple-element.63), channel_id=1, source_target_pairs={{0,4},{4,0},{8,12},{12,8},{1,5},{5,1},{9,13},{13,9},{2,6},{6,2},{1... | collective-permute-start | bytes 2359304 | tf_op jit(solution)/shard_map/ppermute | solution.py:101
  78.7 19.9 %collective-permute-start.4 = (bf16[512,768]{1,0:T(8,128)(2,1)}, bf16[512,768]{1,0:T(8,128)(2,1)}, u32[]{:S(2)}, u32[]{:S(2)}) collective-permute-start(bf16[512,768]{1,0:T(8,128)(2,1)} %add_convert_fusion.5), channel_id=1, source_target_pairs={{0,8},{4,12},{8,0},{12,4},{1,9},{5,13},{9,1},{13,5},{2,10},{6,14},... | collective-permute-start | bytes 2359304 | tf_op jit(solution)/shard_map/ppermute | solution.py:101
  107.9 3.7 collective-permute-start.9
  110.8 13.8 %collective-permute-start.6 = (bf16[512,256]{1,0:T(8,128)(2,1)}, bf16[512,256]{1,0:T(8,128)(2,1)}, u32[]{:S(2)}, u32[]{:S(2)}) collective-permute-start(bf16[512,256]{1,0:T(8,128)(2,1)} %bitcast.145), channel_id=1, source_target_pairs={{0,8},{4,12},{8,0},{12,4},{1,9},{5,13},{9,1},{13,5},{2,10},{6,14},... | collective-permute-start | bytes 786440 | tf_op jit(solution)/shard_map/ppermute | solution.py:101
  124.1 4.6 %collective-permute-start.11 = (bf16[512,768]{1,0:T(8,128)(2,1)}, bf16[512,768]{1,0:T(8,128)(2,1)}, u32[]{:S(2)}, u32[]{:S(2)}) collective-permute-start(bf16[512,768]{1,0:T(8,128)(2,1)} %get-tuple-element.62), channel_id=1, source_target_pairs={{0,4},{4,0},{8,12},{12,8},{1,5},{5,1},{9,13},{13,9},{2,6},{6,2},{1... | collective-permute-start | bytes 2359304 | tf_op jit(solution)/shard_map/ppermute | solution.py:101
  124.1 3.0 collective-permute-start.5
  124.6 2.9 collective-permute-start.7
  124.6 11.0 %collective-permute-start.10 = (bf16[512,768]{1,0:T(8,128)(2,1)}, bf16[512,768]{1,0:T(8,128)(2,1)}, u32[]{:S(2)}, u32[]{:S(2)}) collective-permute-start(bf16[512,768]{1,0:T(8,128)(2,1)} %get-tuple-element.61), channel_id=1, source_target_pairs={{0,4},{4,0},{8,12},{12,8},{1,5},{5,1},{9,13},{13,9},{2,6},{6,2},{1... | collective-permute-start | bytes 2359304 | tf_op jit(solution)/shard_map/ppermute | solution.py:101
  131.1 19.9 %collective-permute-start.12 = (bf16[512,768]{1,0:T(8,128)(2,1)}, bf16[512,768]{1,0:T(8,128)(2,1)}, u32[]{:S(2)}, u32[]{:S(2)}) collective-permute-start(bf16[512,768]{1,0:T(8,128)(2,1)} %add_convert_fusion.3), channel_id=1, source_target_pairs={{0,8},{4,12},{8,0},{12,4},{1,9},{5,13},{9,1},{13,5},{2,10},{6,14},... | collective-permute-start | bytes 2359304 | tf_op jit(solution)/shard_map/ppermute | solution.py:101
  135.5 95.2 %reduce-scatter.6.cloned.1.call-start = ((), (), s32[]{:S(2)}) async-start(), calls=%async_computation.6 | async-start | bytes 1966080 | tf_op jit(solution)/shard_map/reduce_scatter | solution.py:214
  159.8 7.6 %collective-permute-start.14 = (bf16[512,256]{1,0:T(8,128)(2,1)S(1)}, bf16[512,256]{1,0:T(8,128)(2,1)S(1)}, u32[]{:S(2)}, u32[]{:S(2)}) collective-permute-start(bf16[512,256]{1,0:T(8,128)(2,1)S(1)} %bitcast.179), channel_id=1, source_target_pairs={{0,8},{4,12},{8,0},{12,4},{1,9},{5,13},{9,1},{13,5},{2,10},{6,14},... | collective-permute-start | bytes 786440 | tf_op jit(solution)/shard_map/ppermute | solution.py:101
  161.3 6.1 %collective-permute-start.13 = (bf16[512,256]{1,0:T(8,128)(2,1)S(1)}, bf16[512,256]{1,0:T(8,128)(2,1)S(1)}, u32[]{:S(2)}, u32[]{:S(2)}) collective-permute-start(bf16[512,256]{1,0:T(8,128)(2,1)S(1)} %bitcast.180), channel_id=1, source_target_pairs={{0,4},{4,0},{8,12},{12,8},{1,5},{5,1},{9,13},{13,9},{2,6},{6,2},{1... | collective-permute-start | bytes 786440 | tf_op jit(solution)/shard_map/ppermute | solution.py:101
  172.0 123.6 %all-gather.8.cloned.1.call-start = ((), (), s32[]{:S(2)}) async-start(), calls=%async_computation.7 | async-start | bytes 1966080 | tf_op jit(solution)/shard_map/all_gather | solution.py:228
  175.9 3.7 collective-permute-start.17
  181.0 22.2 %collective-permute-start.18 = (bf16[128,1536]{1,0:T(8,128)(2,1)S(1)}, bf16[128,1536]{1,0:T(8,128)(2,1)S(1)}, u32[]{:S(2)}, u32[]{:S(2)}) collective-permute-start(bf16[128,1536]{1,0:T(8,128)(2,1)S(1)} %bitcast.163), channel_id=1, source_target_pairs={{0,1},{1,2},{2,3},{3,0},{4,5},{5,6},{6,7},{7,4},{8,9},{9,10},{10,1... | collective-permute-start | bytes 1179656 | tf_op jit(solution)/shard_map/ppermute | solution.py:127
  181.6 47.8 %collective-permute-start.19 = (bf16[128,1536]{1,0:T(8,128)(2,1)S(1)}, bf16[128,1536]{1,0:T(8,128)(2,1)S(1)}, u32[]{:S(2)}, u32[]{:S(2)}) collective-permute-start(bf16[128,1536]{1,0:T(8,128)(2,1)S(1)} %bitcast.164), channel_id=1, source_target_pairs={{0,2},{1,3},{2,0},{3,1},{4,6},{5,7},{6,4},{7,5},{8,10},{9,11},{10,... | collective-permute-start | bytes 1179656 | tf_op jit(solution)/shard_map/ppermute | solution.py:127
  183.1 46.3 %collective-permute-start.20 = (bf16[128,1536]{1,0:T(8,128)(2,1)S(1)}, bf16[128,1536]{1,0:T(8,128)(2,1)S(1)}, u32[]{:S(2)}, u32[]{:S(2)}) collective-permute-start(bf16[128,1536]{1,0:T(8,128)(2,1)S(1)} %bitcast.165), channel_id=1, source_target_pairs={{0,3},{1,0},{2,1},{3,2},{4,7},{5,4},{6,5},{7,6},{8,11},{9,8},{10,9... | collective-permute-start | bytes 1179656 | tf_op jit(solution)/shard_map/ppermute | solution.py:127
  234.3 3.6 collective-permute-start.22
  249.6 132.9 %reduce-scatter.8.cloned.1.call-start = ((), (), s32[]{:S(2)}) async-start(), calls=%async_computation.8 | async-start | bytes 983040 | tf_op jit(solution)/shard_map/reduce_scatter | solution.py:269
  249.6 6.2 %collective-permute-start.23 = (bf16[128,3072]{1,0:T(8,128)(2,1)}, bf16[128,3072]{1,0:T(8,128)(2,1)}, u32[]{:S(2)}, u32[]{:S(2)}) collective-permute-start(bf16[128,3072]{1,0:T(8,128)(2,1)} %get-tuple-element.59), channel_id=1, source_target_pairs={{0,4},{4,0},{8,12},{12,8},{1,5},{5,1},{9,13},{13,9},{2,6},{6,2},{1... | collective-permute-start | bytes 2359304 | tf_op jit(solution)/shard_map/ppermute | solution.py:101
  254.4 19.9 %collective-permute-start.25 = (bf16[128,3072]{1,0:T(8,128)(2,1)}, bf16[128,3072]{1,0:T(8,128)(2,1)}, u32[]{:S(2)}, u32[]{:S(2)}) collective-permute-start(bf16[128,3072]{1,0:T(8,128)(2,1)} %add_convert_fusion.1), channel_id=1, source_target_pairs={{0,8},{4,12},{8,0},{12,4},{1,9},{5,13},{9,1},{13,5},{2,10},{6,14},... | collective-permute-start | bytes 2359304 | tf_op jit(solution)/shard_map/ppermute | solution.py:101
  277.4 26.6 %collective-permute-start.27 = (bf16[128,3072]{1,0:T(8,128)(2,1)}, bf16[128,3072]{1,0:T(8,128)(2,1)}, u32[]{:S(2)}, u32[]{:S(2)}) collective-permute-start(bf16[128,3072]{1,0:T(8,128)(2,1)} %fusion.33), channel_id=1, source_target_pairs={{0,8},{4,12},{8,0},{12,4},{1,9},{5,13},{9,1},{13,5},{2,10},{6,14},... | collective-permute-start | bytes 2359304 | tf_op jit(solution)/shard_map/ppermute | solution.py:101
  306.0 4.7 %collective-permute-start.26 = (bf16[128,3072]{1,0:T(8,128)(2,1)}, bf16[128,3072]{1,0:T(8,128)(2,1)S(1)}, u32[]{:S(2)}, u32[]{:S(2)}) collective-permute-start(bf16[128,3072]{1,0:T(8,128)(2,1)} %fusion.33), channel_id=1, source_target_pairs={{0,4},{4,0},{8,12},{12,8},{1,5},{5,1},{9,13},{13,9},{2,6},{6,2},{1... | collective-permute-start | bytes 2359304 | tf_op jit(solution)/shard_map/ppermute | solution.py:101
  306.5 4.2 %collective-permute-start.28 = (bf16[128,3072]{1,0:T(8,128)(2,1)}, bf16[128,3072]{1,0:T(8,128)(2,1)S(1)}, u32[]{:S(2)}, u32[]{:S(2)}) collective-permute-start(bf16[128,3072]{1,0:T(8,128)(2,1)} %collective-permute-done.27), channel_id=1, source_target_pairs={{0,4},{4,0},{8,12},{12,8},{1,5},{5,1},{9,13},{13,9},{2,6},{6,2},{1... | collective-permute-start | bytes 2359304 | tf_op jit(solution)/shard_map/ppermute | solution.py:101
  306.6 5.9 %collective-permute-start.29 = (bf16[128,3072]{1,0:T(8,128)(2,1)}, bf16[128,3072]{1,0:T(8,128)(2,1)S(1)}, u32[]{:S(2)}, u32[]{:S(2)}) collective-permute-start(bf16[128,3072]{1,0:T(8,128)(2,1)} %get-tuple-element.57), channel_id=1, source_target_pairs={{0,4},{4,0},{8,12},{12,8},{1,5},{5,1},{9,13},{13,9},{2,6},{6,2},{1... | collective-permute-start | bytes 2359304 | tf_op jit(solution)/shard_map/ppermute | solution.py:101
  309.2 19.6 %collective-permute-start.31 = (bf16[128,3072]{1,0:T(8,128)(2,1)S(1)}, bf16[128,3072]{1,0:T(8,128)(2,1)S(1)}, u32[]{:S(2)}, u32[]{:S(2)}) collective-permute-start(bf16[128,3072]{1,0:T(8,128)(2,1)S(1)} %add_convert_fusion), channel_id=1, source_target_pairs={{0,8},{4,12},{8,0},{12,4},{1,9},{5,13},{9,1},{13,5},{2,10},{6,14},... | collective-permute-start | bytes 2359304 | tf_op jit(solution)/shard_map/ppermute | solution.py:101
  329.6 18.8 %collective-permute-start.33 = (bf16[128,3072]{1,0:T(8,128)(2,1)S(1)}, bf16[128,3072]{1,0:T(8,128)(2,1)S(1)}, u32[]{:S(2)}, u32[]{:S(2)}) collective-permute-start(bf16[128,3072]{1,0:T(8,128)(2,1)S(1)} %fusion.41), channel_id=1, source_target_pairs={{0,8},{4,12},{8,0},{12,4},{1,9},{5,13},{9,1},{13,5},{2,10},{6,14},... | collective-permute-start | bytes 2359304 | tf_op jit(solution)/shard_map/ppermute | solution.py:101
  340.1 8.9 %collective-permute-start.32 = (bf16[128,3072]{1,0:T(8,128)(2,1)S(1)}, bf16[128,3072]{1,0:T(8,128)(2,1)S(1)}, u32[]{:S(2)}, u32[]{:S(2)}) collective-permute-start(bf16[128,3072]{1,0:T(8,128)(2,1)S(1)} %fusion.41), channel_id=1, source_target_pairs={{0,4},{4,0},{8,12},{12,8},{1,5},{5,1},{9,13},{13,9},{2,6},{6,2},{1... | collective-permute-start | bytes 2359304 | tf_op jit(solution)/shard_map/ppermute | solution.py:101
  (27 other events, 342.1 us)
Sparse Core Ops, SparseCore 0:
  12.4 39.7 all-gather.5
  54.4 36.0 all-gather.3
  135.7 33.4 reduce-scatter.3
  172.1 58.5 reduce-scatter.5
  249.7 45.9 all-gather.7
  358.0 24.4 reduce-scatter.7
where the time goes:
time: 396 us; the launch traced here: 391 us
  waiting for transfers between devices  208 us (53%)
  matrix products  56.3 us (14%)
  local copies, waits for them, and re-layouts  46.1 us (12%)
  other arithmetic  41.6 us (11%)
  starting transfers between devices  25.3 us (6%)
  between operations  14.2 us (4%)
    ppermute x32, waiting for transfers between devices, swap_row(): return lax.ppermute(value, 'row', [(r, r ^ distance) for r in range(size)])  103 us
    ppermute x3, waiting for transfers between devices, shift_col(): lax.ppermute(value, 'col', [(c, (c + distance) % size) for c in range(siz...  44.1 us
    reduce_scatter x1, waiting for transfers between devices, head_layer(): mlp = lax.psum_scatter(total, 'col', scatter_dimension=0, tiled=True)  24.6 us
    ppermute x32, starting transfers between devices, swap_row(): return lax.ppermute(value, 'row', [(r, r ^ distance) for r in range(size)])  20.8 us
    all_gather x2, waiting for transfers between devices, head_layer(): gathered = [lax.all_gather(x, 'col', axis=0, tiled=True) for x in x_parts]  19.3 us
    dot_general x2, matrix products, project(): jnp.dot(first, w_flat, preferred_element_type=jnp.float32).astype(BF)  18.8 us
    all_gather x1, waiting for transfers between devices, residual(): return (mixed, lax.all_gather(second, 'col', axis=0, tiled=True))  16.8 us
    unnamed x39, local copies, waits for them, and re-layouts  16.8 us
  transfers between devices with their start and end apart: 41, of which 26 were waited for; matrix products, arithmetic and copies ran while one was open for 27% of the time, Pallas kernels for 0%

commit v1 on v0

--- a/solution.py
+++ b/solution.py
@@ -6,6 +6,28 @@
 D = 6144
 HEAD_DIM = 128
 eps = 1e-06
+
+
+def laid_out(blocks, dim):
+    shape = list(blocks.shape[1:])
+    shape[dim] *= blocks.shape[0]
+    return jnp.moveaxis(blocks, 0, dim).reshape(shape)
+
+
+def collected_by_bits(x, axis):
+    devices = lax.axis_size(axis)
+    tiles = x[None]
+    for level in range(devices.bit_length() - 1):
+        bit = 1 << level
+        partner_block = lax.ppermute(tiles, axis, [(i, i ^ bit) for i in range(devices)])
+        both = jnp.stack([tiles, partner_block])
+        upper = lax.axis_index(axis) >> level & 1
+        tiles = jnp.where(upper == 0, both, both[::-1]).reshape(-1, *x.shape)
+    return tiles
+
+
+def doubled_up(x, axis, dim):
+    return laid_out(collected_by_bits(x, axis), dim)
 
 
 def normalize(values, shift, scale):
@@ -225,7 +247,7 @@
             seconds[-1], second = lax.optimization_barrier((seconds[-1], second))
         if g < GROUPS - 1:
             return (mixed, gather_col(second).reshape(tokens, feat_rows))
-        return (mixed, lax.all_gather(second, "col", axis=0, tiled=True))
+        return (mixed, doubled_up(second, "col", 0))
 
     def expand(g, second_all):
         partial = jnp.dot(second_all, w_up, preferred_element_type=jnp.float32).astype(BF)

time: 396 us -> 411 us (1.038)
  starting transfers between devices: 25.3 us -> 36.8 us
    ppermute x0 -> x2, waiting for transfers between devices: none -> 32.1 us  [collected_by_bits(): lax.ppermute(tiles, axis, [(i, i ^ bit) for i in range(devices)])]
    all_gather x1 -> x0, waiting for transfers between devices: 16.8 us -> none  [residual(): return (mixed, lax.all_gather(second, 'col', axis=0, tiled=True))]
    ppermute x0 -> x2, starting transfers between devices: none -> 11.8 us  [collected_by_bits(): lax.ppermute(tiles, axis, [(i, i ^ bit) for i in range(devices)])]
    ppermute x32, waiting for transfers between devices: 103 us -> 93.4 us  [swap_row(): return lax.ppermute(value, 'row', [(r, r ^ distance) for r in range(size)])]
    unnamed x39 -> x51, local copies, waits for them, and re-layouts: 16.8 us -> 18.9 us
  transfers between devices with their start and end apart: 41 -> 42, of which waited for: 26 -> 27; matrix products, arithmetic and copies ran while one was open for 27% -> 27% of each run, Pallas kernels for 0% -> 0%
where the time goes in v1:
time: 411 us; the launch traced here: 407 us
  waiting for transfers between devices  211 us (51%)
  matrix products  57.2 us (14%)
  local copies, waits for them, and re-layouts  48.4 us (12%)
  other arithmetic  39.1 us (10%)
  starting transfers between devices  36.8 us (9%)
  between operations  14 us (3%)
    ppermute x32, waiting for transfers between devices, swap_row(): return lax.ppermute(value, 'row', [(r, r ^ distance) for r in range(size)])  93.4 us
    ppermute x3, waiting for transfers between devices, shift_col(): lax.ppermute(value, 'col', [(c, (c + distance) % size) for c in range(siz...  44.1 us
    ppermute x2, waiting for transfers between devices, collected_by_bits(): lax.ppermute(tiles, axis, [(i, i ^ bit) for i in range(devices)])  32.1 us
    reduce_scatter x1, waiting for transfers between devices, head_layer(): mlp = lax.psum_scatter(total, 'col', scatter_dimension=0, tiled=True)  22.1 us
    ppermute x32, starting transfers between devices, swap_row(): return lax.ppermute(value, 'row', [(r, r ^ distance) for r in range(size)])  20.6 us
    all_gather x2, waiting for transfers between devices, head_layer(): gathered = [lax.all_gather(x, 'col', axis=0, tiled=True) for x in x_parts]  19.3 us
    unnamed x51, local copies, waits for them, and re-layouts  18.9 us
    dot_general x2, matrix products, project(): jnp.dot(first, w_flat, preferred_element_type=jnp.float32).astype(BF)  18.8 us
  transfers between devices with their start and end apart: 42, of which 27 were waited for; matrix products, arithmetic and copies ran while one was open for 27% of the time, Pallas kernels for 0%

profile of v1, /device:TPU:0, one launch (start us, length us, event | category | flops | bytes accessed | tf_op | source)
XLA Modules:
  0.0 406.7 jit_solution(15372540942541372390)
XLA Ops:
  6.5 2.5 reshape.360
  12.3 12.7 %copy.32 = bf16[1536,3,1024]{0,2,1:T(8,128)(2,1)} copy(bf16[1536,3,1024]{2,0,1:T(8,128)(2,1)} %param.10) | data formatting | bytes 18874368 | tf_op args[2]
  24.9 7.9 %copy.33 = bf16[1536,4,3,256]{0,3,2,1:T(8,128)(2,1)} copy(bf16[1536,4,3,256]{0,3,1,2:T(8,128)(2,1)} %bitcast.155) | data formatting | bytes 18874368 | tf_op jit(solution)/shard_map/transpose | solution.py:210
  32.9 19.3 %all-gather.5.cloned.1.call-done = bf16[512,1536]{1,0:T(8,128)(2,1)} async-done(((bf16[128,1536]{1,0:T(8,128)(2,1)}), bf16[512,1536]{1,0:T(8,128)(2,1)}) %all-gather.5.cloned.1.call-update) | async-done | bytes 1572880 | tf_op jit(solution)/shard_map/all_gather | solution.py:217
  59.1 2.7 fusion.4
  61.8 9.6 %convolution_convert_fusion.3 = bf16[512,3072]{1,0:T(8,128)(2,1)S(1)} fusion(bf16[512,1536]{1,0:T(8,128)(2,1)S(1)} %fusion.4, bf16[1536,3072]{0,1:T(8,128)(2,1)} %bitcast.161), kind=kOutput, calls=%fused_computation.9 | convolution fusion | flops 4833411072 | bytes 14155776 | tf_op jit(solution)/shard_map/dot_general | solution.py:225
  76.2 2.5 add_convert_fusion.5
  80.2 18.4 %collective-permute-done.4 = bf16[512,768]{1,0:T(8,128)(2,1)} collective-permute-done((bf16[512,768]{1,0:T(8,128)(2,1)}, bf16[512,768]{1,0:T(8,128)(2,1)}, u32[]{:S(2)}, u32[]{:S(2)}) %collective-permute-start.4) | collective-permute-done | bytes 786464 | tf_op jit(solution)/shard_map/ppermute | solution.py:123
  98.6 2.8 add_convert_fusion.4
  101.4 2.7 reshape.365
  112.8 9.1 %convolution_convert_fusion.2 = bf16[512,3072]{1,0:T(8,128)(2,1)S(1)} fusion(bf16[512,1536]{1,0:T(8,128)(2,1)S(1)} %fusion.9, bf16[1536,3072]{0,1:T(8,128)(2,1)} %bitcast.162), kind=kOutput, calls=%fused_computation.8 | convolution fusion | flops 4833411072 | bytes 14155776 | tf_op jit(solution)/shard_map/dot_general | solution.py:225
  128.7 2.4 add_convert_fusion.3
  132.6 3.0 convolution_convert_fusion.5
  135.6 15.4 %collective-permute-done.12 = bf16[512,768]{1,0:T(8,128)(2,1)} collective-permute-done((bf16[512,768]{1,0:T(8,128)(2,1)}, bf16[512,768]{1,0:T(8,128)(2,1)}, u32[]{:S(2)}, u32[]{:S(2)}) %collective-permute-start.12) | collective-permute-done | bytes 786464 | tf_op jit(solution)/shard_map/ppermute | solution.py:123
  151.0 2.8 add_convert_fusion.2
  153.8 2.9 reshape.370
  161.4 6.1 %collective-permute-done.14 = bf16[512,256]{1,0:T(8,128)(2,1)S(1)} collective-permute-done((bf16[512,256]{1,0:T(8,128)(2,1)S(1)}, bf16[512,256]{1,0:T(8,128)(2,1)S(1)}, u32[]{:S(2)}, u32[]{:S(2)}) %collective-permute-start.14) | collective-permute-done | bytes 262176 | tf_op jit(solution)/shard_map/ppermute | solution.py:123
  169.0 3.0 convolution_convert_fusion.4
  177.5 2.1 collective-permute-done.17
  183.2 2.2 collective-permute-start.20
  185.4 17.9 %collective-permute-done.18 = bf16[128,1536]{1,0:T(8,128)(2,1)S(1)} collective-permute-done((bf16[128,1536]{1,0:T(8,128)(2,1)S(1)}, bf16[128,1536]{1,0:T(8,128)(2,1)S(1)}, u32[]{:S(2)}, u32[]{:S(2)}) %collective-permute-start.18) | collective-permute-done | bytes 393248 | tf_op jit(solution)/shard_map/ppermute | solution.py:149
  203.4 26.2 %collective-permute-done.19 = bf16[128,1536]{1,0:T(8,128)(2,1)S(1)} collective-permute-done((bf16[128,1536]{1,0:T(8,128)(2,1)S(1)}, bf16[128,1536]{1,0:T(8,128)(2,1)S(1)}, u32[]{:S(2)}, u32[]{:S(2)}) %collective-permute-start.19) | collective-permute-done | bytes 393248 | tf_op jit(solution)/shard_map/ppermute | solution.py:149
  239.5 10.3 %collective-permute-start.23 = (bf16[1,128,1536]{2,1,0:T(8,128)(2,1)S(1)}, bf16[1,128,1536]{2,1,0:T(8,128)(2,1)S(1)}, u32[]{:S(2)}, u32[]{:S(2)}) collective-permute-start(bf16[1,128,1536]{2,1,0:T(8,128)(2,1)S(1)} %bitcast.181), channel_id=1, source_target_pairs={{0,1},{1,0},{2,3},{3,2},{4,5},{5,4},{6,7},{7,6},{8,9},{9,8},{10,11... | collective-permute-start | bytes 1179656 | tf_op jit(solution)/shard_map/ppermute | solution.py:22
  249.8 8.1 %convolution_convert_fusion.1 = bf16[512,3072]{1,0:T(8,128)(2,1)S(1)} fusion(bf16[512,1536]{1,0:T(8,128)(2,1)} %bitcast.171, bf16[1536,3072]{1,0:T(8,128)(2,1)} %param.12), kind=kOutput, calls=%fused_computation.7 | convolution fusion | flops 4833411072 | bytes 14155776 | tf_op jit(solution)/shard_map/dot_general | solution.py:253
  265.4 32.1 %collective-permute-done.24 = bf16[2,128,1536]{2,1,0:T(8,128)(2,1)S(1)} collective-permute-done((bf16[2,128,1536]{2,1,0:T(8,128)(2,1)S(1)}, bf16[2,128,1536]{2,1,0:T(8,128)(2,1)S(1)}, u32[]{:S(2)}, u32[]{:S(2)}) %collective-permute-start.24) | collective-permute-done | bytes 786464 | tf_op jit(solution)/shard_map/ppermute | solution.py:22
  303.9 9.1 %convolution_convert_fusion = bf16[512,3072]{1,0:T(8,128)(2,1)S(1)} fusion(bf16[512,1536]{1,0:T(8,128)(2,1)S(1)} %bitcast.178, bf16[1536,3072]{1,0:T(8,128)(2,1)} %param.12), kind=kOutput, calls=%fused_computation.6 | convolution fusion | flops 4833411072 | bytes 14155776 | tf_op jit(solution)/shard_map/dot_general | solution.py:253
  313.0 8.9 %collective-permute-done.29 = bf16[128,3072]{1,0:T(8,128)(2,1)S(1)} collective-permute-done((bf16[128,3072]{1,0:T(8,128)(2,1)S(1)}, bf16[128,3072]{1,0:T(8,128)(2,1)S(1)}, u32[]{:S(2)}, u32[]{:S(2)}) %collective-permute-start.29) | collective-permute-done | bytes 786464 | tf_op jit(solution)/shard_map/ppermute | solution.py:123
  329.2 17.7 %collective-permute-done.33 = bf16[128,3072]{1,0:T(8,128)(2,1)S(1)} collective-permute-done((bf16[128,3072]{1,0:T(8,128)(2,1)S(1)}, bf16[128,3072]{1,0:T(8,128)(2,1)S(1)}, u32[]{:S(2)}, u32[]{:S(2)}) %collective-permute-start.33) | collective-permute-done | bytes 786464 | tf_op jit(solution)/shard_map/ppermute | solution.py:123
  349.2 8.9 %fusion.10 = f32[512,1536]{1,0:T(8,128)S(1)} fusion(bf16[3072,1536]{1,0:T(8,128)(2,1)} %param.14, bf16[128,3072]{1,0:T(8,128)(2,1)S(1)} %get-tuple-element.48, bf16[128,3072]{1,0:T(8,128)(2,1)S(1)} %get-tuple-element.49, bf16[128,3072]{1,0:T(8,128)(2,1)S(1)} %get-tuple-element.50, bf16[128,3072]{1,0:T(8,128)(2,1)S(1)} %get-tuple-element.47), kind=kOutput, calls=%fused_computation.20 | convolution fusion | flops 4844421120 | bytes 15728640 | tf_op jit(solution)/shard_map/dot_general | solution.py:263
  358.2 8.3 %collective-permute-done.35 = bf16[128,3072]{1,0:T(8,128)(2,1)S(1)} collective-permute-done((bf16[128,3072]{1,0:T(8,128)(2,1)S(1)}, bf16[128,3072]{1,0:T(8,128)(2,1)S(1)}, u32[]{:S(2)}, u32[]{:S(2)}) %collective-permute-start.35) | collective-permute-done | bytes 786464 | tf_op jit(solution)/shard_map/ppermute | solution.py:123
  369.1 5.0 %fusion.18 = f32[512,1536]{1,0:T(8,128)S(1)} fusion(bf16[3072,1536]{1,0:T(8,128)(2,1)S(1)} %bitcast.217, bf16[128,3072]{1,0:T(8,128)(2,1)S(1)} %get-tuple-element.54, bf16[128,3072]{1,0:T(8,128)(2,1)S(1)} %get-tuple-element.55, bf16[128,3072]{1,0:T(8,128)(2,1)S(1)} %get-tuple-element.56, bf16[128,3072]{1,0:T(8,128)(2,1)S(1)} %get-tuple-element.53), kind=kOutput, calls=%fused_computation.28 | convolution fusion | flops 4844421120 | bytes 15728640 | tf_op jit(solution)/shard_map/dot_general | solution.py:263
  375.9 22.1 %reduce-scatter.8.cloned.1.call-done = bf16[64,1536]{1,0:T(8,128)(2,1)} async-done(((bf16[256,1536]{1,0:T(8,128)(2,1)}), bf16[64,1536]{1,0:T(8,128)(2,1)}) %reduce-scatter.8.cloned.1.call-update) | async-done | bytes 196624 | tf_op jit(solution)/shard_map/reduce_scatter | solution.py:291
  (207 shorter events, 87.8 us)
Async XLA Ops:
  6.5 45.6 %all-gather.5.cloned.1.call-start = ((), (), s32[]{:S(2)}) async-start(), calls=%async_computation.4 | async-start | bytes 1966080 | tf_op jit(solution)/shard_map/all_gather | solution.py:217
  12.2 89.2 %all-gather.3.cloned.1.call-start = ((), (), s32[]{:S(2)}) async-start(), calls=%async_computation.3 | async-start | bytes 1966080 | tf_op jit(solution)/shard_map/all_gather | solution.py:217
  54.3 118.5 %reduce-scatter.4.cloned.1.call-start = ((), (), s32[]{:S(2)}) async-start(), calls=%async_computation.5 | async-start | bytes 1966080 | tf_op jit(solution)/shard_map/reduce_scatter | solution.py:236
  55.4 3.7 collective-permute-start.1
  73.6 6.6 %collective-permute-start.2 = (bf16[512,768]{1,0:T(8,128)(2,1)}, bf16[512,768]{1,0:T(8,128)(2,1)}, u32[]{:S(2)}, u32[]{:S(2)}) collective-permute-start(bf16[512,768]{1,0:T(8,128)(2,1)} %get-tuple-element.63), channel_id=1, source_target_pairs={{0,4},{4,0},{8,12},{12,8},{1,5},{5,1},{9,13},{13,9},{2,6},{6,2},{1... | collective-permute-start | bytes 2359304 | tf_op jit(solution)/shard_map/ppermute | solution.py:123
  78.7 19.9 %collective-permute-start.4 = (bf16[512,768]{1,0:T(8,128)(2,1)}, bf16[512,768]{1,0:T(8,128)(2,1)}, u32[]{:S(2)}, u32[]{:S(2)}) collective-permute-start(bf16[512,768]{1,0:T(8,128)(2,1)} %add_convert_fusion.5), channel_id=1, source_target_pairs={{0,8},{4,12},{8,0},{12,4},{1,9},{5,13},{9,1},{13,5},{2,10},{6,14},... | collective-permute-start | bytes 2359304 | tf_op jit(solution)/shard_map/ppermute | solution.py:123
  107.9 3.7 collective-permute-start.9
  110.8 13.8 %collective-permute-start.6 = (bf16[512,256]{1,0:T(8,128)(2,1)}, bf16[512,256]{1,0:T(8,128)(2,1)}, u32[]{:S(2)}, u32[]{:S(2)}) collective-permute-start(bf16[512,256]{1,0:T(8,128)(2,1)} %bitcast.154), channel_id=1, source_target_pairs={{0,8},{4,12},{8,0},{12,4},{1,9},{5,13},{9,1},{13,5},{2,10},{6,14},... | collective-permute-start | bytes 786440 | tf_op jit(solution)/shard_map/ppermute | solution.py:123
  124.1 4.6 %collective-permute-start.11 = (bf16[512,768]{1,0:T(8,128)(2,1)}, bf16[512,768]{1,0:T(8,128)(2,1)}, u32[]{:S(2)}, u32[]{:S(2)}) collective-permute-start(bf16[512,768]{1,0:T(8,128)(2,1)} %get-tuple-element.62), channel_id=1, source_target_pairs={{0,4},{4,0},{8,12},{12,8},{1,5},{5,1},{9,13},{13,9},{2,6},{6,2},{1... | collective-permute-start | bytes 2359304 | tf_op jit(solution)/shard_map/ppermute | solution.py:123
  124.1 3.0 collective-permute-start.5
  124.6 11.0 %collective-permute-start.10 = (bf16[512,768]{1,0:T(8,128)(2,1)}, bf16[512,768]{1,0:T(8,128)(2,1)}, u32[]{:S(2)}, u32[]{:S(2)}) collective-permute-start(bf16[512,768]{1,0:T(8,128)(2,1)} %get-tuple-element.61), channel_id=1, source_target_pairs={{0,4},{4,0},{8,12},{12,8},{1,5},{5,1},{9,13},{13,9},{2,6},{6,2},{1... | collective-permute-start | bytes 2359304 | tf_op jit(solution)/shard_map/ppermute | solution.py:123
  131.1 19.9 %collective-permute-start.12 = (bf16[512,768]{1,0:T(8,128)(2,1)}, bf16[512,768]{1,0:T(8,128)(2,1)}, u32[]{:S(2)}, u32[]{:S(2)}) collective-permute-start(bf16[512,768]{1,0:T(8,128)(2,1)} %add_convert_fusion.3), channel_id=1, source_target_pairs={{0,8},{4,12},{8,0},{12,4},{1,9},{5,13},{9,1},{13,5},{2,10},{6,14},... | collective-permute-start | bytes 2359304 | tf_op jit(solution)/shard_map/ppermute | solution.py:123
  135.6 95.3 %reduce-scatter.6.cloned.1.call-start = ((), (), s32[]{:S(2)}) async-start(), calls=%async_computation.6 | async-start | bytes 1966080 | tf_op jit(solution)/shard_map/reduce_scatter | solution.py:236
  159.8 7.6 %collective-permute-start.14 = (bf16[512,256]{1,0:T(8,128)(2,1)S(1)}, bf16[512,256]{1,0:T(8,128)(2,1)S(1)}, u32[]{:S(2)}, u32[]{:S(2)}) collective-permute-start(bf16[512,256]{1,0:T(8,128)(2,1)S(1)} %bitcast.192), channel_id=1, source_target_pairs={{0,8},{4,12},{8,0},{12,4},{1,9},{5,13},{9,1},{13,5},{2,10},{6,14},... | collective-permute-start | bytes 786440 | tf_op jit(solution)/shard_map/ppermute | solution.py:123
  161.3 6.1 %collective-permute-start.13 = (bf16[512,256]{1,0:T(8,128)(2,1)S(1)}, bf16[512,256]{1,0:T(8,128)(2,1)S(1)}, u32[]{:S(2)}, u32[]{:S(2)}) collective-permute-start(bf16[512,256]{1,0:T(8,128)(2,1)S(1)} %bitcast.193), channel_id=1, source_target_pairs={{0,4},{4,0},{8,12},{12,8},{1,5},{5,1},{9,13},{13,9},{2,6},{6,2},{1... | collective-permute-start | bytes 786440 | tf_op jit(solution)/shard_map/ppermute | solution.py:123
  172.1 226.0 %reduce-scatter.8.cloned.1.call-start = ((), (), s32[]{:S(2)}) async-start(), calls=%async_computation.7 | async-start | bytes 983040 | tf_op jit(solution)/shard_map/reduce_scatter | solution.py:291
  175.9 3.7 collective-permute-start.17
  181.1 22.2 %collective-permute-start.18 = (bf16[128,1536]{1,0:T(8,128)(2,1)S(1)}, bf16[128,1536]{1,0:T(8,128)(2,1)S(1)}, u32[]{:S(2)}, u32[]{:S(2)}) collective-permute-start(bf16[128,1536]{1,0:T(8,128)(2,1)S(1)} %bitcast.172), channel_id=1, source_target_pairs={{0,1},{1,2},{2,3},{3,0},{4,5},{5,6},{6,7},{7,4},{8,9},{9,10},{10,1... | collective-permute-start | bytes 1179656 | tf_op jit(solution)/shard_map/ppermute | solution.py:149
  181.7 47.8 %collective-permute-start.19 = (bf16[128,1536]{1,0:T(8,128)(2,1)S(1)}, bf16[128,1536]{1,0:T(8,128)(2,1)S(1)}, u32[]{:S(2)}, u32[]{:S(2)}) collective-permute-start(bf16[128,1536]{1,0:T(8,128)(2,1)S(1)} %bitcast.173), channel_id=1, source_target_pairs={{0,2},{1,3},{2,0},{3,1},{4,6},{5,7},{6,4},{7,5},{8,10},{9,11},{10,... | collective-permute-start | bytes 1179656 | tf_op jit(solution)/shard_map/ppermute | solution.py:149
  183.2 46.3 %collective-permute-start.20 = (bf16[128,1536]{1,0:T(8,128)(2,1)S(1)}, bf16[128,1536]{1,0:T(8,128)(2,1)S(1)}, u32[]{:S(2)}, u32[]{:S(2)}) collective-permute-start(bf16[128,1536]{1,0:T(8,128)(2,1)S(1)} %bitcast.174), channel_id=1, source_target_pairs={{0,3},{1,0},{2,1},{3,2},{4,7},{5,4},{6,5},{7,6},{8,11},{9,8},{10,9... | collective-permute-start | bytes 1179656 | tf_op jit(solution)/shard_map/ppermute | solution.py:149
  234.4 3.6 collective-permute-start.22
  239.5 20.5 %collective-permute-start.23 = (bf16[1,128,1536]{2,1,0:T(8,128)(2,1)S(1)}, bf16[1,128,1536]{2,1,0:T(8,128)(2,1)S(1)}, u32[]{:S(2)}, u32[]{:S(2)}) collective-permute-start(bf16[1,128,1536]{2,1,0:T(8,128)(2,1)S(1)} %bitcast.181), channel_id=1, source_target_pairs={{0,1},{1,0},{2,3},{3,2},{4,5},{5,4},{6,7},{7,6},{8,9},{9,8},{10,11... | collective-permute-start | bytes 1179656 | tf_op jit(solution)/shard_map/ppermute | solution.py:22
  260.3 37.2 %collective-permute-start.24 = (bf16[2,128,1536]{2,1,0:T(8,128)(2,1)S(1)}, bf16[2,128,1536]{2,1,0:T(8,128)(2,1)S(1)}, u32[]{:S(2)}, u32[]{:S(2)}) collective-permute-start(bf16[2,128,1536]{2,1,0:T(8,128)(2,1)S(1)} %get-tuple-element.78), channel_id=1, source_target_pairs={{0,2},{1,3},{2,0},{3,1},{4,6},{5,7},{6,4},{7,5},{8,10},{9,11},{10,... | collective-permute-start | bytes 2359304 | tf_op jit(solution)/shard_map/ppermute | solution.py:22
  261.8 38.2 %collective-permute-start.25 = (bf16[128,3072]{1,0:T(8,128)(2,1)}, bf16[128,3072]{1,0:T(8,128)(2,1)S(1)}, u32[]{:S(2)}, u32[]{:S(2)}) collective-permute-start(bf16[128,3072]{1,0:T(8,128)(2,1)} %get-tuple-element.59), channel_id=1, source_target_pairs={{0,4},{4,0},{8,12},{12,8},{1,5},{5,1},{9,13},{13,9},{2,6},{6,2},{1... | collective-permute-start | bytes 2359304 | tf_op jit(solution)/shard_map/ppermute | solution.py:123
  263.8 36.1 %collective-permute-start.27 = (bf16[128,3072]{1,0:T(8,128)(2,1)S(1)}, bf16[128,3072]{1,0:T(8,128)(2,1)S(1)}, u32[]{:S(2)}, u32[]{:S(2)}) collective-permute-start(bf16[128,3072]{1,0:T(8,128)(2,1)S(1)} %add_convert_fusion.1), channel_id=1, source_target_pairs={{0,8},{4,12},{8,0},{12,4},{1,9},{5,13},{9,1},{13,5},{2,10},{6,14},... | collective-permute-start | bytes 2359304 | tf_op jit(solution)/shard_map/ppermute | solution.py:123
  302.3 19.6 %collective-permute-start.29 = (bf16[128,3072]{1,0:T(8,128)(2,1)S(1)}, bf16[128,3072]{1,0:T(8,128)(2,1)S(1)}, u32[]{:S(2)}, u32[]{:S(2)}) collective-permute-start(bf16[128,3072]{1,0:T(8,128)(2,1)S(1)} %fusion.33), channel_id=1, source_target_pairs={{0,8},{4,12},{8,0},{12,4},{1,9},{5,13},{9,1},{13,5},{2,10},{6,14},... | collective-permute-start | bytes 2359304 | tf_op jit(solution)/shard_map/ppermute | solution.py:123
  324.2 4.6 %collective-permute-start.28 = (bf16[128,3072]{1,0:T(8,128)(2,1)}, bf16[128,3072]{1,0:T(8,128)(2,1)S(1)}, u32[]{:S(2)}, u32[]{:S(2)}) collective-permute-start(bf16[128,3072]{1,0:T(8,128)(2,1)} %copy-done.8), channel_id=1, source_target_pairs={{0,4},{4,0},{8,12},{12,8},{1,5},{5,1},{9,13},{13,9},{2,6},{6,2},{1... | collective-permute-start | bytes 2359304 | tf_op jit(solution)/shard_map/ppermute | solution.py:123
  324.7 4.1 collective-permute-start.30
  324.8 4.3 %collective-permute-start.31 = (bf16[128,3072]{1,0:T(8,128)(2,1)}, bf16[128,3072]{1,0:T(8,128)(2,1)S(1)}, u32[]{:S(2)}, u32[]{:S(2)}) collective-permute-start(bf16[128,3072]{1,0:T(8,128)(2,1)} %get-tuple-element.57), channel_id=1, source_target_pairs={{0,4},{4,0},{8,12},{12,8},{1,5},{5,1},{9,13},{13,9},{2,6},{6,2},{1... | collective-permute-start | bytes 2359304 | tf_op jit(solution)/shard_map/ppermute | solution.py:123
  327.3 19.6 %collective-permute-start.33 = (bf16[128,3072]{1,0:T(8,128)(2,1)S(1)}, bf16[128,3072]{1,0:T(8,128)(2,1)S(1)}, u32[]{:S(2)}, u32[]{:S(2)}) collective-permute-start(bf16[128,3072]{1,0:T(8,128)(2,1)S(1)} %add_convert_fusion), channel_id=1, source_target_pairs={{0,8},{4,12},{8,0},{12,4},{1,9},{5,13},{9,1},{13,5},{2,10},{6,14},... | collective-permute-start | bytes 2359304 | tf_op jit(solution)/shard_map/ppermute | solution.py:123
  347.7 18.8 %collective-permute-start.35 = (bf16[128,3072]{1,0:T(8,128)(2,1)S(1)}, bf16[128,3072]{1,0:T(8,128)(2,1)S(1)}, u32[]{:S(2)}, u32[]{:S(2)}) collective-permute-start(bf16[128,3072]{1,0:T(8,128)(2,1)S(1)} %fusion.41), channel_id=1, source_target_pairs={{0,8},{4,12},{8,0},{12,4},{1,9},{5,13},{9,1},{13,5},{2,10},{6,14},... | collective-permute-start | bytes 2359304 | tf_op jit(solution)/shard_map/ppermute | solution.py:123
  358.1 8.9 %collective-permute-start.34 = (bf16[128,3072]{1,0:T(8,128)(2,1)S(1)}, bf16[128,3072]{1,0:T(8,128)(2,1)S(1)}, u32[]{:S(2)}, u32[]{:S(2)}) collective-permute-start(bf16[128,3072]{1,0:T(8,128)(2,1)S(1)} %fusion.41), channel_id=1, source_target_pairs={{0,4},{4,0},{8,12},{12,8},{1,5},{5,1},{9,13},{13,9},{2,6},{6,2},{1... | collective-permute-start | bytes 2359304 | tf_op jit(solution)/shard_map/ppermute | solution.py:123
  (34 other events, 344.5 us)
Sparse Core Ops, SparseCore 0:
  12.3 39.7 all-gather.4
  54.4 36.0 all-gather.2
  135.7 33.4 reduce-scatter.3
  172.2 58.6 reduce-scatter.5
  376.1 21.9 reduce-scatter.7
